TPU v7x, 32 devices: a whole 2x2x4 slice. The times are simulated.
32 devices in a mesh: rx: 4 (over y, x), chirp: 8 (over z, core).
Axes of the slice: x: 2, y: 2, z: 4, core: 2. Of those that a mesh axis runs over, the one named last changes fastest.
Arguments:
- samples: bfloat16 [2, 128, 128, 4096], P(None, None, 'rx', 'chirp'), may hold values from -6 to 6
- tx_offsets: int32 [12], replicated, may hold values from 0 to 3840, as said below
- band_owner: int32 [16], replicated, may hold values from 0 to 3, as said below
- beam_weights: bfloat16 [2, 256, 1536], replicated, may hold values from -0.109375 to 0.109375
Outputs:
- tile_store: bfloat16 [48, 2, 256, 2048], P('rx', None, None, 'chirp')
Inputs may be any that keep to these rules, and one draw needn't show every extreme that they name: `tx_offsets`: each offset is 256 times a Doppler slot of 0 to 15; transmitters use different slots, and slots 0 and 15 are always used. `band_owner`: at most 12 bands share an owner, and one owner has exactly 12.
All inputs are finite; a program needn't handle non-finite values.
Results may differ from a plain program's by a relative error of at most 0.007.
Values may be sent and summed in bfloat16 or wider, within the bound.
No kernel may reach another device: no remote copies, remote signals or barrier semaphores. Data moves between devices by JAX's collectives and lax.ppermute only.
A program may use at most 192 MiB of HBM per device.

v0:
```python
from functools import partial
import math
import jax
import jax.numpy as jnp
from jax import lax
from jax.sharding import PartitionSpec as P

K1 = 64
K2 = 64
SLOTS = 16


def dft_pair(size):
    indices = jnp.arange(size, dtype=jnp.int32)
    product = indices[:, None] * indices[None, :] % size
    phase_angle = product.astype(jnp.float32) * (-2.0 * math.pi / size)
    scale = 1.0 / math.sqrt(size)
    return (
        (jnp.cos(phase_angle) * scale).astype(jnp.bfloat16),
        (jnp.sin(phase_angle) * scale).astype(jnp.bfloat16),
    )


def twiddle_table():
    outer = jnp.arange(K1, dtype=jnp.int32)[:, None]
    inner = jnp.arange(K2, dtype=jnp.int32)[None, :]
    phase_angle = (outer * inner % (K1 * K2)).astype(jnp.float32) * (-2.0 * math.pi / (K1 * K2))
    return (jnp.cos(phase_angle), jnp.sin(phase_angle))


def spectrum_of(real_part, imag_part, row_count):
    mixing = partial(jnp.einsum, preferred_element_type=jnp.float32)
    split_re = real_part.reshape(row_count, K1, K2)
    split_im = imag_part.reshape(row_count, K1, K2)
    table_re, table_im = dft_pair(K1)
    section_re = mixing("kn,rnm->rkm", table_re, split_re) - mixing(
        "kn,rnm->rkm", table_im, split_im
    )
    section_im = mixing("kn,rnm->rkm", table_re, split_im) + mixing(
        "kn,rnm->rkm", table_im, split_re
    )
    twist_re, twist_im = twiddle_table()
    turned_re = (section_re * twist_re - section_im * twist_im).astype(jnp.bfloat16)
    turned_im = (section_re * twist_im + section_im * twist_re).astype(jnp.bfloat16)
    final_re, final_im = dft_pair(K2)
    out_re = mixing("qm,rkm->rqk", final_re, turned_re) - mixing("qm,rkm->rqk", final_im, turned_im)
    out_im = mixing("qm,rkm->rqk", final_re, turned_im) + mixing("qm,rkm->rqk", final_im, turned_re)
    return (
        out_re.reshape(row_count, K1 * K2).astype(jnp.bfloat16),
        out_im.reshape(row_count, K1 * K2).astype(jnp.bfloat16),
    )


def shards(samples, tx_offsets, band_owner, beam_weights):
    owners = lax.axis_size("rx")
    band_count = band_owner.shape[0]
    capacity = 3 * band_count // owners
    tx_count = tx_offsets.shape[0]
    bin_count = K1 * K2
    speed_bins = bin_count // SLOTS
    band_width = speed_bins // band_count
    starts = (tx_offsets - speed_bins // 2) % bin_count
    sender = jnp.arange(tx_count, dtype=jnp.int32)[:, None]
    speed = jnp.arange(speed_bins, dtype=jnp.int32)[None, :] - speed_bins // 2
    phase_angle = (sender * speed).astype(jnp.float32) * (-2.0 * math.pi / (tx_count * speed_bins))
    cos_part = jnp.cos(phase_angle)[:, None, None, :]
    sin_part = jnp.sin(phase_angle)[:, None, None, :]
    pieces = lax.all_to_all(samples, "chirp", split_axis=1, concat_axis=3, tiled=True)
    bin_rows = pieces.shape[1]
    item_count = pieces.shape[2]
    spec_re, spec_im = spectrum_of(
        pieces[0].reshape(bin_rows * item_count, bin_count),
        pieces[1].reshape(bin_rows * item_count, bin_count),
        bin_rows * item_count,
    )
    joined = jnp.stack([spec_re, spec_im]).reshape(2, bin_rows, item_count, bin_count)
    double = jnp.concatenate([joined, joined], axis=3)

    def take_band(begin_at):
        return lax.dynamic_slice_in_dim(double, begin_at, speed_bins, 3)

    picked = jax.vmap(take_band)(starts)
    got_re = picked[:, 0].astype(jnp.float32)
    got_im = picked[:, 1].astype(jnp.float32)
    demux_re = got_re * cos_part - got_im * sin_part
    demux_im = got_re * sin_part + got_im * cos_part
    demuxed = jnp.stack([demux_re, demux_im]).astype(jnp.bfloat16)
    demuxed = demuxed.transpose(0, 1, 3, 2, 4)
    rx_local = demuxed.shape[2]
    bin_rows = demuxed.shape[3]
    tile_width = bin_rows * band_width
    tiles = demuxed.reshape(2, tx_count, rx_local, bin_rows, band_count, band_width)
    tiles = tiles.transpose(4, 0, 1, 2, 3, 5).reshape(band_count, 2, tx_count, rx_local, tile_width)
    counter = jnp.arange(band_count, dtype=jnp.int32)
    same_owner = band_owner[:, None] == band_owner[None, :]
    earlier = counter[None, :] < counter[:, None]
    band_rank = jnp.sum((same_owner & earlier).astype(jnp.int32), axis=1)
    weight_re = beam_weights[0]
    weight_im = beam_weights[1]
    slot_ids = band_owner * capacity + band_rank
    choose = (slot_ids[None, :] == jnp.arange(owners * capacity, dtype=jnp.int32)[:, None]).astype(
        jnp.bfloat16
    )
    outgoing = jnp.dot(
        choose, tiles.reshape(band_count, -1), preferred_element_type=jnp.float32
    ).astype(jnp.bfloat16)
    outgoing = outgoing.reshape(owners, capacity, 2, tx_count, rx_local, tile_width)
    slots = lax.all_to_all(outgoing, "rx", split_axis=0, concat_axis=4, tiled=True)[0]
    item_count = slots.shape[0]
    channels = slots.reshape(item_count, 2, slots.shape[2] * slots.shape[3], slots.shape[4])
    mixing = partial(jnp.einsum, preferred_element_type=jnp.float32)
    beam_re = mixing("bc,scm->sbm", weight_re, channels[:, 0]) - mixing(
        "bc,scm->sbm", weight_im, channels[:, 1]
    )
    beam_im = mixing("bc,scm->sbm", weight_re, channels[:, 1]) + mixing(
        "bc,scm->sbm", weight_im, channels[:, 0]
    )
    return jnp.stack([beam_re, beam_im], axis=1).astype(jnp.bfloat16)


def solution(mesh):
    placed = (P(None, None, "rx", "chirp"), P(), P(), P())
    return jax.shard_map(
        shards, mesh=mesh, in_specs=placed, out_specs=P("rx", None, None, "chirp"), check_vma=False
    )
```

profile of v0, /device:TPU:0, one launch (start us, length us, event | category | flops | bytes accessed | tf_op | source)
XLA Modules:
  0.0 832.5 jit_solution(5319038525160731027)
XLA Ops:
  0.0 8.3 copy.56
  8.3 6.5 all-to-all-start
  15.7 183.0 %all-to-all-done = bf16[2,128,32,512]{3,2,0,1:T(8,128)(2,1)} async-done(((bf16[2,128,32,512]{3,2,0,1:T(8,128)(2,1)}), bf16[2,128,32,512]{3,2,0,1:T(8,128)(2,1)}, u32[]{:S(2)}, u32[]{:S(2)}) %all-to-all-start) | async-done | bytes 8388640 | tf_op jit(solution)/shard_map/all_to_all | solution.py:68
  198.7 15.4 %copy.96 = bf16[2,8,16,32,512]{4,1,3,2,0:T(8,128)(2,1)} copy(bf16[2,8,16,32,512]{4,3,0,2,1:T(8,128)(2,1)} %bitcast.1) | data formatting | bytes 16777216 | tf_op jit(solution)/shard_map/all_to_all | solution.py:68
  214.1 5.9 fusion.107
  220.0 11.2 %reshape_reshape_squeeze.7 = bf16[512,64,64]{2,1,0:T(8,128)(2,1)} reshape(bf16[1,16,32,8,512]{4,3,2,1,0:T(8,128)(2,1)} %get-tuple-element.24) | data formatting | bytes 8388608 | tf_op jit(solution)/shard_map/reshape;reshape;squeeze | solution.py:34
  231.2 12.2 %copy.59 = bf16[512,64,64]{0,1,2:T(8,128)(2,1)} copy(bf16[512,64,64]{2,1,0:T(8,128)(2,1)} %reshape_reshape_squeeze.7) | data formatting | bytes 8388608 | tf_op jit(solution)/shard_map/reshape;reshape;squeeze | solution.py:34
  243.4 6.9 fusion.55
  250.3 4.6 fusion.59
  254.9 11.2 %reshape_reshape_squeeze.6 = bf16[512,64,64]{2,1,0:T(8,128)(2,1)} reshape(bf16[1,16,32,8,512]{4,3,2,1,0:T(8,128)(2,1)} %get-tuple-element.23) | data formatting | bytes 8388608 | tf_op jit(solution)/shard_map/reshape;reshape;squeeze | solution.py:33
  266.1 12.0 %copy.58 = bf16[512,64,64]{0,1,2:T(8,128)(2,1)} copy(bf16[512,64,64]{2,1,0:T(8,128)(2,1)} %reshape_reshape_squeeze.6) | data formatting | bytes 8388608 | tf_op jit(solution)/shard_map/reshape;reshape;squeeze | solution.py:33
  278.1 6.9 fusion.53
  285.0 12.4 %fusion.8 = (bf16[512,64,64]{0,1,2:T(8,128)(2,1)}, bf16[512,64,64]{0,1,2:T(8,128)(2,1)S(1)}) fusion(f32[64,64]{0,1:T(8,128)S(1)} %copy.63, f32[64,64]{0,1:T(8,128)S(1)} %copy.60, f32[64,512,64]{1,0,2:T(8,128)} %fusion.59, f32[64,512,64]{1,0,2:T(8,128)} %fusion.53, f32[64,512,64]{1,0,2:T(8,128)} %fusion.55, bf16[512,64,64]{0,1,2:T(8,128)(2,1)S(1)} %copy-done), kind=kOutput, calls=%fused_computation.24 | convolution fusion | flops 289472512 | bytes 37781504 | tf_op jit(solution)/shard_map/kn,rnm->rkm/dot_general | solution.py:36
  297.4 5.6 fusion.12
  303.0 8.8 %fusion.14 = f32[512,64,64]{0,2,1:T(8,128)} fusion(bf16[512,64,64]{0,1,2:T(8,128)(2,1)S(1)} %get-tuple-element.22), kind=kOutput, calls=%fused_computation.30 | convolution fusion | flops 268500992 | bytes 12582912 | tf_op jit(solution)/shard_map/qm,rkm->rqk/dot_general | solution.py:47
  311.8 8.1 fusion.10
  319.9 15.6 %copy.66 = bf16[512,64,64]{2,1,0:T(8,128)(2,1)} copy(bf16[512,64,64]{0,1,2:T(8,128)(2,1)} %fusion.10) | data formatting | bytes 8388608 | tf_op jit(solution)/shard_map/convert_element_type | solution.py:49
  335.5 12.0 %convert_element_type.170 = bf16[1,16,32,4096]{3,2,1,0:T(8,128)(2,1)} reshape(bf16[512,64,64]{2,1,0:T(8,128)(2,1)} %copy.66) | data formatting | bytes 8388608 | tf_op jit(solution)/shard_map/convert_element_type | solution.py:49
  347.6 12.4 %fusion.11 = bf16[512,64,64]{0,1,2:T(8,128)(2,1)} fusion(f32[512,64,64]{0,2,1:T(8,128)} %fusion.14, bf16[512,64,64]{0,1,2:T(8,128)(2,1)} %get-tuple-element.21), kind=kOutput, calls=%fused_computation.27 | convolution fusion | flops 272695296 | bytes 16777216 | tf_op jit(solution)/shard_map/qm,rkm->rqk/dot_general | solution.py:47
  359.9 15.8 %copy.69 = bf16[512,64,64]{2,1,0:T(8,128)(2,1)} copy(bf16[512,64,64]{0,1,2:T(8,128)(2,1)} %fusion.11) | data formatting | bytes 8388608 | tf_op jit(solution)/shard_map/convert_element_type | solution.py:50
  375.7 12.1 %convert_element_type.173 = bf16[1,16,32,4096]{3,2,1,0:T(8,128)(2,1)} reshape(bf16[512,64,64]{2,1,0:T(8,128)(2,1)} %copy.69) | data formatting | bytes 8388608 | tf_op jit(solution)/shard_map/convert_element_type | solution.py:50
  387.8 14.0 %maximum_maximum_fusion = bf16[2,16,32,8192]{3,2,1,0:T(8,128)(2,1)} fusion(bf16[1,16,32,4096]{3,2,1,0:T(8,128)(2,1)} %convert_element_type.173, bf16[1,16,32,4096]{3,2,1,0:T(8,128)(2,1)} %convert_element_type.170), kind=kLoop, calls=%fused_computation.3 | loop fusion | flops 67108864 | bytes 25165824 | tf_op jit(solution)/shard_map/concatenate | solution.py:77
  401.8 41.0 %while.1 = (s32[]{:T(128)}, bf16[2,16,32,8192]{3,2,1,0:T(8,128)(2,1)}, s32[12,4]{0,1:T(4,128)S(1)}, bf16[12,2,16,32,256]{4,3,2,0,1:T(8,128)(2,1)}, s32[]{:T(128)}) while((s32[]{:T(128)}, bf16[2,16,32,8192]{3,2,1,0:T(8,128)(2,1)}, s32[12,4]{0,1:T(4,128)S(1)}, bf16[12,2,16,32,256]{4,3,2,0,1:T(8,128)(2,1)}, s32[]{:T(128)}) %tuple.20), condition=%wide.while_cond, body=%wide.while_body.sunk | while | flops 2 | bytes 1049705 | solution.py:80
  402.4 2.8 bitcast_dynamic-update-slice_fusion.2
  405.8 2.8 bitcast_dynamic-update-slice_fusion.2
  409.2 2.8 bitcast_dynamic-update-slice_fusion.2
  412.6 2.8 bitcast_dynamic-update-slice_fusion.2
  416.1 2.8 bitcast_dynamic-update-slice_fusion.2
  419.5 2.8 bitcast_dynamic-update-slice_fusion.2
  422.9 2.8 bitcast_dynamic-update-slice_fusion.2
  426.3 2.8 bitcast_dynamic-update-slice_fusion.2
  429.7 2.8 bitcast_dynamic-update-slice_fusion.2
  433.2 2.8 bitcast_dynamic-update-slice_fusion.2
  436.6 2.8 bitcast_dynamic-update-slice_fusion.2
  440.0 2.8 bitcast_dynamic-update-slice_fusion.2
  442.8 4.0 fusion.5
  446.8 3.2 pad_maximum_fusion
  450.0 21.0 %copy.72 = bf16[2,12,16,32,256]{3,4,2,1,0:T(8,128)(2,1)} copy(bf16[2,12,16,32,256]{4,3,2,1,0:T(8,128)(2,1)} %pad_maximum_fusion) | data formatting | bytes 12582912 | tf_op jit(solution)/shard_map/stack | solution.py:87
  471.0 54.6 %copy.73 = bf16[16,2,12,32,16,16]{5,4,3,2,1,0:T(8,128)(2,1)} copy(bf16[16,2,12,32,16,16]{3,5,0,4,2,1:T(8,128)(2,1)} %bitcast.110) | data formatting | bytes 12582912 | tf_op jit(solution)/shard_map/transpose | solution.py:93
  525.6 45.0 %reshape_reshape.3 = bf16[16,196608]{1,0:T(8,128)(2,1)} reshape(bf16[16,2,12,32,16,16]{5,4,3,2,1,0:T(8,128)(2,1)} %copy.73) | data formatting | bytes 12582912 | tf_op jit(solution)/shard_map/reshape;reshape | solution.py:105
  570.6 11.8 %convolution_convert_fusion = bf16[48,196608]{1,0:T(8,128)(2,1)} fusion(bf16[16,196608]{1,0:T(8,128)(2,1)} %reshape_reshape.3, s32[16]{0:T(128)S(1)} %multiply_add_fusion), kind=kOutput, calls=%fused_computation.2 | convolution fusion | flops 311427840 | bytes 25165888 | tf_op jit(solution)/shard_map/dot_general | solution.py:104
  582.5 11.5 %copy.82 = bf16[6,8,768,256]{3,2,1,0:T(8,128)(2,1)S(1)} copy(bf16[6,8,768,256]{3,1,2,0:T(8,128)(2,1)} %bitcast.111) | data formatting | bytes 37748736
  593.9 208.6 %all_to_all.30 = bf16[4,12,2,12,32,256]{5,4,3,2,1,0:T(8,128)(2,1)S(1)} all-to-all(bf16[4,12,2,12,32,256]{5,4,3,2,1,0:T(8,128)(2,1)S(1)} %bitcast.112), channel_id=1, replica_groups=mesh['rx'=4,'chirp'=8] {'rx'}, dimensions={0} | all-to-all | bytes 37748736 | tf_op jit(solution)/shard_map/all_to_all | solution.py:108
  802.5 6.6 copy.74
  809.1 8.2 fusion.1
  819.3 2.7 fusion
  822.0 4.4 fusion.24
  829.3 2.8 copy.77
  (53 shorter events, 13.2 us)
Async XLA Ops:
  8.3 7.0 copy-start.6
  8.3 7.2 copy-start.5
  8.3 190.4 %all-to-all-start = ((bf16[2,128,32,512]{3,2,0,1:T(8,128)(2,1)}), bf16[2,128,32,512]{3,2,0,1:T(8,128)(2,1)}, u32[]{:S(2)}, u32[]{:S(2)}) async-start(bf16[2,128,32,512]{3,2,0,1:T(8,128)(2,1)} %copy.56), calls=%async_computation | async-start | bytes 16777216 | tf_op jit(solution)/shard_map/all_to_all | solution.py:68
  243.3 6.9 copy-start.1
  278.1 6.9 copy-start
  303.0 8.8 %copy-start.2 = (bf16[512,64,64]{0,1,2:T(8,128)(2,1)S(1)}, bf16[512,64,64]{0,1,2:T(8,128)(2,1)}, u32[]{:S(2)}) copy-start(bf16[512,64,64]{0,1,2:T(8,128)(2,1)} %get-tuple-element.21) | copy-start | bytes 12582916
  802.5 6.6 copy-start.4
  809.1 10.2 %copy-start.3 = (bf16[4,12,2,12,32,256]{5,4,0,3,2,1:T(8,128)(2,1)S(1)}, bf16[4,12,2,12,32,256]{5,4,0,3,2,1:T(8,128)(2,1)}, u32[]{:S(2)}) copy-start(bf16[4,12,2,12,32,256]{5,4,0,3,2,1:T(8,128)(2,1)} %copy.74) | copy-start | bytes 56623108
where the time goes:
time: 846 us; the launch traced here: 832 us
  local copies, waits for them, and re-layouts  316 us (37%)
  blocking collectives  209 us (25%)
  waiting for transfers between devices  183 us (22%)
  matrix products  95.3 us (11%)
  other arithmetic  22.2 us (3%)
    all_to_all x1, blocking collectives, shards(): lax.all_to_all(outgoing, 'rx', split_axis=0, concat_axis=4, tiled=True)[0]  209 us
    all_to_all x1, waiting for transfers between devices, shards(): lax.all_to_all(samples, 'chirp', split_axis=1, concat_axis=3, tiled=True)  183 us
    transpose x1, local copies, waits for them, and re-layouts, shards(): tiles.transpose(4, 0, 1, 2, 3, 5)  54.6 us
    another operation x1, local copies, waits for them, and re-layouts, shards(): tiles.reshape(band_count, -1)  45 us
    gather x36, local copies, waits for them, and re-layouts  41 us
    convert_element_type x2, local copies, waits for them, and re-layouts, spectrum_of(): out_im.reshape(row_count, K1 * K2).astype(jnp.bfloat16)  27.9 us
    convert_element_type x2, local copies, waits for them, and re-layouts, spectrum_of(): out_re.reshape(row_count, K1 * K2).astype(jnp.bfloat16)  27.7 us
    another operation x2, local copies, waits for them, and re-layouts, spectrum_of(): split_im = imag_part.reshape(row_count, K1, K2)  23.4 us
  transfers between devices with their start and end apart: 1, of which 1 were waited for; matrix products, arithmetic and copies ran while one was open for 0% of the time, Pallas kernels for 0%

commit v1 on v0

--- a/solution.py
+++ b/solution.py
@@ -65,7 +65,12 @@
     phase_angle = (sender * speed).astype(jnp.float32) * (-2.0 * math.pi / (tx_count * speed_bins))
     cos_part = jnp.cos(phase_angle)[:, None, None, :]
     sin_part = jnp.sin(phase_angle)[:, None, None, :]
-    pieces = lax.all_to_all(samples, "chirp", split_axis=1, concat_axis=3, tiled=True)
+    pieces = jnp.concatenate(
+        lax.all_to_all(
+            jnp.stack(jnp.split(samples, lax.axis_size("chirp"), axis=1)), "chirp", 0, 0
+        ),
+        axis=3,
+    )
     bin_rows = pieces.shape[1]
     item_count = pieces.shape[2]
     spec_re, spec_im = spectrum_of(

time: 846 us -> 851 us (level)
    all_to_all x1 -> x0, local copies, waits for them, and re-layouts: 15.4 us -> none  [shards(): lax.all_to_all(samples, 'chirp', split_axis=1, concat_axis=3, tiled=True)]
    unnamed x16 -> x24, local copies, waits for them, and re-layouts: 21.8 us -> 29.9 us
where the time goes in v1:
time: 851 us; the launch traced here: 837 us
  local copies, waits for them, and re-layouts  321 us (38%)
  blocking collectives  209 us (25%)
  waiting for transfers between devices  183 us (22%)
  matrix products  95.1 us (11%)
  other arithmetic  22.2 us (3%)
    all_to_all x1, blocking collectives, shards(): lax.all_to_all(outgoing, 'rx', split_axis=0, concat_axis=4, tiled=True)[0]  209 us
    all_to_all x1, waiting for transfers between devices, shards(): lax.all_to_all(jnp.stack(jnp.split(samples, lax.axis_size('chirp'), axis=...  183 us
    transpose x1, local copies, waits for them, and re-layouts, shards(): tiles.transpose(4, 0, 1, 2, 3, 5)  54.6 us
    another operation x1, local copies, waits for them, and re-layouts, shards(): tiles.reshape(band_count, -1)  45 us
    gather x36, local copies, waits for them, and re-layouts  41.5 us
    unnamed x24, local copies, waits for them, and re-layouts  29.9 us
    convert_element_type x2, local copies, waits for them, and re-layouts, spectrum_of(): out_im.reshape(row_count, K1 * K2).astype(jnp.bfloat16)  27.9 us
    convert_element_type x2, local copies, waits for them, and re-layouts, spectrum_of(): out_re.reshape(row_count, K1 * K2).astype(jnp.bfloat16)  27.7 us
  transfers between devices with their start and end apart: 1, of which 1 were waited for; matrix products, arithmetic and copies ran while one was open for 0% of the time, Pallas kernels for 0%

profile of v1, /device:TPU:0, one launch (start us, length us, event | category | flops | bytes accessed | tf_op | source)
XLA Modules:
  0.0 837.0 jit_solution(191411274853438230)
XLA Ops:
  18.7 6.5 all-to-all-start
  26.1 183.0 %all-to-all-done = bf16[8,2,16,32,512]{4,3,2,1,0:T(8,128)(2,1)} async-done(((bf16[8,2,16,32,512]{4,3,2,1,0:T(8,128)(2,1)}), bf16[8,2,16,32,512]{4,3,2,1,0:T(8,128)(2,1)}, u32[]{:S(2)}, u32[]{:S(2)}) %all-to-all-start) | async-done | bytes 8388640 | tf_op jit(solution)/shard_map/all_to_all | solution.py:69
  209.1 5.3 fusion.109
  214.5 4.9 copy.57
  219.3 11.2 %reshape_reshape_squeeze.6 = bf16[512,64,64]{2,1,0:T(8,128)(2,1)} reshape(bf16[1,16,32,8,512]{4,3,2,1,0:T(8,128)(2,1)} %copy.57) | data formatting | bytes 8388608 | tf_op jit(solution)/shard_map/reshape;reshape;squeeze | solution.py:33
  230.5 12.1 %copy.58 = bf16[512,64,64]{0,1,2:T(8,128)(2,1)} copy(bf16[512,64,64]{2,1,0:T(8,128)(2,1)} %reshape_reshape_squeeze.6) | data formatting | bytes 8388608 | tf_op jit(solution)/shard_map/reshape;reshape;squeeze | solution.py:33
  242.6 6.9 fusion.55
  249.5 4.6 fusion.59
  254.1 4.9 copy.59
  259.0 11.2 %reshape_reshape_squeeze.7 = bf16[512,64,64]{2,1,0:T(8,128)(2,1)} reshape(bf16[1,16,32,8,512]{4,3,2,1,0:T(8,128)(2,1)} %copy.59) | data formatting | bytes 8388608 | tf_op jit(solution)/shard_map/reshape;reshape;squeeze | solution.py:34
  270.2 12.2 %copy.60 = bf16[512,64,64]{0,1,2:T(8,128)(2,1)} copy(bf16[512,64,64]{2,1,0:T(8,128)(2,1)} %reshape_reshape_squeeze.7) | data formatting | bytes 8388608 | tf_op jit(solution)/shard_map/reshape;reshape;squeeze | solution.py:34
  282.3 6.9 fusion.53
  289.2 12.3 %fusion.1 = (bf16[512,64,64]{0,1,2:T(8,128)(2,1)}, bf16[512,64,64]{0,1,2:T(8,128)(2,1)S(1)}) fusion(f32[64,64]{0,1:T(8,128)S(1)} %copy.64, f32[64,64]{0,1:T(8,128)S(1)} %copy.61, f32[512,64,64]{0,2,1:T(8,128)} %fusion.55, f32[512,64,64]{0,2,1:T(8,128)} %fusion.59, f32[512,64,64]{0,2,1:T(8,128)} %fusion.53, bf16[512,64,64]{0,1,2:T(8,128)(2,1)S(1)} %copy-done), kind=kOutput, calls=%fused_computation.9 | convolution fusion | flops 289472512 | bytes 37781504 | tf_op jit(solution)/shard_map/kn,rnm->rkm/dot_general | solution.py:39
  301.5 5.6 fusion.14
  307.1 8.8 %fusion.16 = f32[512,64,64]{0,2,1:T(8,128)} fusion(bf16[512,64,64]{0,1,2:T(8,128)(2,1)S(1)} %get-tuple-element.22), kind=kOutput, calls=%fused_computation.33 | convolution fusion | flops 268500992 | bytes 12582912 | tf_op jit(solution)/shard_map/qm,rkm->rqk/dot_general | solution.py:47
  315.9 8.1 fusion.12
  323.9 15.6 %copy.67 = bf16[512,64,64]{2,1,0:T(8,128)(2,1)} copy(bf16[512,64,64]{0,1,2:T(8,128)(2,1)} %fusion.12) | data formatting | bytes 8388608 | tf_op jit(solution)/shard_map/convert_element_type | solution.py:49
  339.6 12.0 %convert_element_type.162 = bf16[1,16,32,4096]{3,2,1,0:T(8,128)(2,1)} reshape(bf16[512,64,64]{2,1,0:T(8,128)(2,1)} %copy.67) | data formatting | bytes 8388608 | tf_op jit(solution)/shard_map/convert_element_type | solution.py:49
  351.6 12.3 %fusion.13 = bf16[512,64,64]{0,1,2:T(8,128)(2,1)} fusion(f32[512,64,64]{0,2,1:T(8,128)} %fusion.16, bf16[512,64,64]{0,1,2:T(8,128)(2,1)} %get-tuple-element.21), kind=kOutput, calls=%fused_computation.30 | convolution fusion | flops 272695296 | bytes 16777216 | tf_op jit(solution)/shard_map/qm,rkm->rqk/dot_general | solution.py:47
  364.0 15.8 %copy.70 = bf16[512,64,64]{2,1,0:T(8,128)(2,1)} copy(bf16[512,64,64]{0,1,2:T(8,128)(2,1)} %fusion.13) | data formatting | bytes 8388608 | tf_op jit(solution)/shard_map/convert_element_type | solution.py:50
  379.8 12.1 %convert_element_type.165 = bf16[1,16,32,4096]{3,2,1,0:T(8,128)(2,1)} reshape(bf16[512,64,64]{2,1,0:T(8,128)(2,1)} %copy.70) | data formatting | bytes 8388608 | tf_op jit(solution)/shard_map/convert_element_type | solution.py:50
  391.9 14.0 %maximum_maximum_fusion = bf16[2,16,32,8192]{3,2,1,0:T(8,128)(2,1)} fusion(bf16[1,16,32,4096]{3,2,1,0:T(8,128)(2,1)} %convert_element_type.165, bf16[1,16,32,4096]{3,2,1,0:T(8,128)(2,1)} %convert_element_type.162), kind=kLoop, calls=%fused_computation.3 | loop fusion | flops 67108864 | bytes 25165824 | tf_op jit(solution)/shard_map/concatenate | solution.py:82
  405.8 41.5 %while.1 = (s32[]{:T(128)}, bf16[2,16,32,8192]{3,2,1,0:T(8,128)(2,1)}, s32[12,4]{0,1:T(4,128)S(1)}, bf16[12,2,16,32,256]{4,3,2,0,1:T(8,128)(2,1)}, s32[]{:T(128)}) while((s32[]{:T(128)}, bf16[2,16,32,8192]{3,2,1,0:T(8,128)(2,1)}, s32[12,4]{0,1:T(4,128)S(1)}, bf16[12,2,16,32,256]{4,3,2,0,1:T(8,128)(2,1)}, s32[]{:T(128)}) %tuple.20), condition=%wide.while_cond, body=%wide.while_body.sunk | while | flops 2 | bytes 1049705 | solution.py:85
  406.5 2.8 bitcast_dynamic-update-slice_fusion.10
  409.9 2.8 bitcast_dynamic-update-slice_fusion.10
  413.4 2.8 bitcast_dynamic-update-slice_fusion.10
  416.8 2.8 bitcast_dynamic-update-slice_fusion.10
  420.3 2.8 bitcast_dynamic-update-slice_fusion.10
  423.8 2.8 bitcast_dynamic-update-slice_fusion.10
  427.2 2.8 bitcast_dynamic-update-slice_fusion.10
  430.7 2.8 bitcast_dynamic-update-slice_fusion.10
  434.2 2.8 bitcast_dynamic-update-slice_fusion.10
  437.6 2.8 bitcast_dynamic-update-slice_fusion.10
  441.1 2.8 bitcast_dynamic-update-slice_fusion.10
  444.5 2.8 bitcast_dynamic-update-slice_fusion.10
  447.3 4.0 fusion.9
  451.4 3.2 pad_maximum_fusion
  454.6 21.0 %copy.73 = bf16[2,12,16,32,256]{3,4,2,1,0:T(8,128)(2,1)} copy(bf16[2,12,16,32,256]{4,3,2,1,0:T(8,128)(2,1)} %pad_maximum_fusion) | data formatting | bytes 12582912 | tf_op jit(solution)/shard_map/stack | solution.py:92
  475.6 54.6 %copy.74 = bf16[16,2,12,32,16,16]{5,4,3,2,1,0:T(8,128)(2,1)} copy(bf16[16,2,12,32,16,16]{3,5,0,4,2,1:T(8,128)(2,1)} %bitcast.137) | data formatting | bytes 12582912 | tf_op jit(solution)/shard_map/transpose | solution.py:98
  530.1 45.0 %reshape_reshape.3 = bf16[16,196608]{1,0:T(8,128)(2,1)} reshape(bf16[16,2,12,32,16,16]{5,4,3,2,1,0:T(8,128)(2,1)} %copy.74) | data formatting | bytes 12582912 | tf_op jit(solution)/shard_map/reshape;reshape | solution.py:110
  575.1 11.8 %convolution_convert_fusion = bf16[48,196608]{1,0:T(8,128)(2,1)} fusion(bf16[16,196608]{1,0:T(8,128)(2,1)} %reshape_reshape.3, s32[16]{0:T(128)S(1)} %multiply_add_fusion), kind=kOutput, calls=%fused_computation.2 | convolution fusion | flops 311427840 | bytes 25165888 | tf_op jit(solution)/shard_map/dot_general | solution.py:109
  587.0 11.5 %copy.83 = bf16[6,8,768,256]{3,2,1,0:T(8,128)(2,1)S(1)} copy(bf16[6,8,768,256]{3,1,2,0:T(8,128)(2,1)} %bitcast.138) | data formatting | bytes 37748736
  598.4 208.6 %all_to_all.20 = bf16[4,12,2,12,32,256]{5,4,3,2,1,0:T(8,128)(2,1)S(1)} all-to-all(bf16[4,12,2,12,32,256]{5,4,3,2,1,0:T(8,128)(2,1)S(1)} %bitcast.139), channel_id=1, replica_groups=mesh['rx'=4,'chirp'=8] {'rx'}, dimensions={0} | all-to-all | bytes 37748736 | tf_op jit(solution)/shard_map/all_to_all | solution.py:113
  807.0 6.6 copy.75
  813.6 8.2 fusion.5
  823.8 2.7 fusion.4
  826.5 4.4 fusion.26
  833.8 2.8 copy.78
  (63 shorter events, 32.4 us)
Async XLA Ops:
  18.7 7.0 copy-start.7
  18.7 7.2 copy-start.6
  18.7 190.4 %all-to-all-start = ((bf16[8,2,16,32,512]{4,3,2,1,0:T(8,128)(2,1)}), bf16[8,2,16,32,512]{4,3,2,1,0:T(8,128)(2,1)}, u32[]{:S(2)}, u32[]{:S(2)}) async-start(bf16[8,2,16,32,512]{4,3,2,1,0:T(8,128)(2,1)} %bitcast_dynamic-update-slice_fusion.1), calls=%async_computation | async-start | bytes 16777216 | tf_op jit(solution)/shard_map/all_to_all | solution.py:69
  242.6 6.9 copy-start.1
  249.5 4.6 copy-start.4
  282.3 6.9 copy-start
  307.1 8.8 %copy-start.2 = (bf16[512,64,64]{0,1,2:T(8,128)(2,1)S(1)}, bf16[512,64,64]{0,1,2:T(8,128)(2,1)}, u32[]{:S(2)}) copy-start(bf16[512,64,64]{0,1,2:T(8,128)(2,1)} %get-tuple-element.21) | copy-start | bytes 12582916
  807.0 6.6 copy-start.5
  813.6 10.2 %copy-start.3 = (bf16[4,12,2,12,32,256]{5,4,0,3,2,1:T(8,128)(2,1)S(1)}, bf16[4,12,2,12,32,256]{5,4,0,3,2,1:T(8,128)(2,1)}, u32[]{:S(2)}) copy-start(bf16[4,12,2,12,32,256]{5,4,0,3,2,1:T(8,128)(2,1)} %copy.75) | copy-start | bytes 56623108
